TPU v7x, 256 devices: a whole 4x4x8 slice. The times are simulated.
256 devices in a mesh: gz: 2 (over core), row: 4 (over x), col: 32 (over z, y).
Axes of the slice: x: 4, y: 4, z: 8, core: 2. Of those that a mesh axis runs over, the one named last changes fastest.
Arguments:
- front_matrix: float32 [4096, 4096], P('row', 'col'), may hold values from -6 to 6
- l_panels: float32 [2, 8, 4, 512, 256], P('gz', None, 'row', 'col'), may hold values from -6 to 6
- l_map: int32 [2, 8, 4, 512], P('gz', None, 'row'), may hold values from 0 to 1024, as said below
- u_panels: float32 [2, 8, 32, 64, 256], P('gz', None, 'col', 'row'), may hold values from -0.375 to 0.375
- u_map: int32 [2, 8, 32, 64], P('gz', None, 'col'), may hold values from 0 to 128, as said below
Outputs:
- updated_front: float32 [4096, 4096], P('row', 'col')
Inputs may be any that keep to these rules, and one draw needn't show every extreme that they name: l_map[z,h,p,:] lists distinct rows of row block p updated by child h of layer z, used slots first, listed block of 128 rows by block, at most 64 rows to a block; unused slots hold 1024; in every child some row block uses all 512 slots. u_map[z,h,q,:] lists distinct columns of column block q updated by child h of layer z, used slots first, listed block of 128 columns by block, at most 64 to a block; unused slots hold 128; in every child some column block uses all 64 slots.
All inputs are finite; a program needn't handle non-finite values.
Results may differ from a plain program's by a relative error of at most 0.0001.
Values sent between devices are 32-bit elements; how exact they have to be, the bound alone decides.
A program may use at most 64 MiB of HBM per device.

v0:
```python
import jax
import jax.numpy as jnp
from jax import lax
from jax.sharding import PartitionSpec as P


def spread_dense(row_panel, row_map, col_dense, row_count):
    targets = jnp.arange(row_count, dtype=jnp.int32)
    narrow = jnp.einsum("hik,hgk->hig", row_panel, col_dense, precision=lax.Precision.HIGHEST)
    row_hot = (row_map[:, :, None] == targets[None, None, :]).astype(jnp.float32)
    return jnp.einsum("hif,hig->fg", row_hot, narrow, precision=lax.Precision.HIGHEST)


def shards(front_matrix, l_panels, l_map, u_panels, u_map):
    row_count, col_count = front_matrix.shape
    row_map = l_map[0, :, 0, :]
    col_map = u_map[0, :, 0, :]
    col_panel = lax.all_gather(u_panels, "row", axis=3, tiled=True)[0, :, 0]
    col_targets = jnp.arange(col_count, dtype=jnp.int32)
    col_hot = (col_map[:, :, None] == col_targets[None, None, :]).astype(jnp.float32)
    col_dense = jnp.einsum("hjg,hjk->hgk", col_hot, col_panel, precision=lax.Precision.HIGHEST)
    row_panel = lax.all_gather(l_panels, "col", axis=3, tiled=True)[0, :, 0]
    update = spread_dense(row_panel, row_map, col_dense, row_count)
    summed = lax.psum(update, "gz")
    return front_matrix - summed


def solution(mesh):
    placed = (
        P("row", "col"),
        P("gz", None, "row", "col", None),
        P("gz", None, "row", None),
        P("gz", None, "col", "row", None),
        P("gz", None, "col", None),
    )
    return jax.shard_map(
        shards, mesh=mesh, in_specs=placed, out_specs=P("row", "col"), check_vma=False
    )
```

profile of v0, /device:TPU:1, one launch (start us, length us, event | category | flops | bytes accessed | tf_op | source)
XLA Modules:
  0.0 145.7 jit_solution(16361774498330991726)
XLA Ops:
  6.5 0.0 all-gather.2.cloned.1.call-start
  6.5 0.7 all-gather.2.cloned.1.call-update
  7.3 0.0 all-reduce.2.cloned.1.call-start
  7.3 0.7 copy.8
  8.0 12.5 %all_gather.6 = f32[1,8,1,64,256]{4,3,2,1,0:T(8,128)S(1)} all-gather(f32[1,8,1,16,256]{4,3,2,1,0:T(8,128)} %param.8), channel_id=1, replica_groups=mesh['gz'=2,'row'=4,'col'=32] {'row'}, dimensions={3}, use_global_device_ids=true | all-gather | bytes 655360 | tf_op jit(solution)/shard_map/all_gather | solution.py:18
  20.6 1.5 %fusion.8 = f32[8,128,256]{2,1,0:T(8,128)S(1)} fusion(f32[1,8,1,64,256]{4,3,2,1,0:T(8,128)S(1)} %all_gather.6, s32[8,64]{1,0:T(8,128)} %bitcast.19), kind=kOutput, calls=%fused_computation.7 | convolution fusion | flops 201392128 | bytes 1574912 | tf_op jit(solution)/shard_map/hjg,hjk->hgk/dot_general | solution.py:21
  22.1 70.8 %all-gather.2.cloned.1.call-done = f32[1,8,1,512,256]{4,3,2,1,0:T(8,128)} async-done(((f32[1,8,1,16,256]{4,3,2,1,0:T(8,128)}), f32[1,8,1,512,256]{4,3,2,1,0:T(8,128)}) %all-gather.2.cloned.1.call-update) | async-done | bytes 4194320 | tf_op jit(solution)/shard_map/all_gather | solution.py:22
  92.9 5.3 %fusion.2 = f32[8,128,512]{1,2,0:T(8,128)S(1)} fusion(f32[8,128,256]{2,1,0:T(8,128)S(1)} %fusion.8, f32[1,8,1,512,256]{4,3,2,1,0:T(8,128)} %all-gather.2.cloned.1.call-done), kind=kOutput, calls=%fused_computation.3 | convolution fusion | flops 1610612736 | bytes 7340032 | tf_op jit(solution)/shard_map/hik,hgk->hig/dot_general | solution.py:9
  98.3 0.0 copy-start
  98.3 8.4 %fusion.5 = f32[1024,128]{1,0:T(8,128)} fusion(f32[8,128,512]{1,2,0:T(8,128)S(1)} %fusion.2, s32[8,512]{1,0:T(8,128)S(1)} %bitcast.18), kind=kOutput, calls=%fused_computation.6 | convolution fusion | flops 6446645248 | bytes 2637824 | tf_op jit(solution)/shard_map/hif,hig->fg/dot_general | solution.py:11
  106.6 0.0 all-reduce.2.cloned.1.call-update
  106.7 30.3 %all-reduce.2.cloned.1.call-done = f32[1024,128]{1,0:T(8,128)} async-done(((f32[1024,128]{1,0:T(8,128)}), f32[1024,128]{1,0:T(8,128)}) %all-reduce.2.cloned.1.call-update) | async-done | bytes 524304 | tf_op jit(solution)/shard_map/psum | solution.py:24
  137.0 0.0 copy-done
  137.0 1.9 %sub.3 = f32[1024,128]{1,0:T(8,128)} subtract(f32[1024,128]{1,0:T(8,128)S(1)} %copy-done, f32[1024,128]{1,0:T(8,128)} %all-reduce.2.cloned.1.call-done) | non-fusion elementwise | flops 131072 | bytes 1572864 | tf_op jit(solution)/shard_map/sub | solution.py:25
Async XLA Ops:
  6.5 86.4 %all-gather.2.cloned.1.call-start = ((), (), s32[]{:S(2)}) async-start(), calls=%async_computation | async-start | bytes 4325376 | tf_op jit(solution)/shard_map/all_gather | solution.py:22
  7.3 129.7 %all-reduce.2.cloned.1.call-start = ((), (), s32[]{:S(2)}) async-start(), calls=%async_computation.1 | async-start | bytes 1048576 | tf_op jit(solution)/shard_map/psum | solution.py:24
  98.3 38.7 %copy-start = (f32[1024,128]{1,0:T(8,128)S(1)}, f32[1024,128]{1,0:T(8,128)}, u32[]{:S(2)}) copy-start(f32[1024,128]{1,0:T(8,128)} %param.5) | copy-start | bytes 1572868
Sparse Core Ops, SparseCore 0:
  9.9 82.9 all-gather.1
  106.8 30.1 all-reduce.1
where the time goes:
time: 146 us
  waiting for transfers between devices  102 us (70%)
  matrix products  15.3 us (10%)
  between operations  13.4 us (9%)
  blocking collectives  12.5 us (9%)
  other arithmetic  1.89 us (1%)
    all_gather x1, waiting for transfers between devices, shards(): row_panel = lax.all_gather(l_panels, 'col', axis=3, tiled=True)[0, :, 0]  70.8 us
    psum x1, waiting for transfers between devices, shards(): summed = lax.psum(update, 'gz')  30.3 us
    all_gather x1, blocking collectives, shards(): col_panel = lax.all_gather(u_panels, 'row', axis=3, tiled=True)[0, :, 0]  12.5 us
    dot_general x1, matrix products, spread_dense(): jnp.einsum('hif,hig->fg', row_hot, narrow, precision=lax.Precision.HIGHEST)  8.37 us
    dot_general x1, matrix products, spread_dense(): jnp.einsum('hik,hgk->hig', row_panel, col_dense, precision=lax.Precision....  5.34 us
  transfers between devices with their start and end apart: 2, of which 2 were waited for; matrix products, arithmetic and copies ran while one was open for 2% of the time, Pallas kernels for 0%

commit v1 on v0

--- a/solution.py
+++ b/solution.py
@@ -2,6 +2,19 @@
 import jax.numpy as jnp
 from jax import lax
 from jax.sharding import PartitionSpec as P
+
+
+def collect(x, axis, dim):
+    ways = lax.axis_size(axis)
+    up = [(d, (d + 1) % ways) for d in range(ways)]
+    down = [(d, (d - 1) % ways) for d in range(ways)]
+    earlier, later = ([x], [x])
+    for _ in range(ways // 2):
+        earlier.append(lax.ppermute(earlier[-1], axis, up))
+    for _ in range((ways - 1) // 2):
+        later.append(lax.ppermute(later[-1], axis, down))
+    line = jnp.concatenate([*earlier[::-1], *later[1:]], axis=dim)
+    return jnp.roll(line, (lax.axis_index(axis) - ways // 2) * x.shape[dim], axis=dim)
 
 
 def spread_dense(row_panel, row_map, col_dense, row_count):
@@ -15,7 +28,7 @@
     row_count, col_count = front_matrix.shape
     row_map = l_map[0, :, 0, :]
     col_map = u_map[0, :, 0, :]
-    col_panel = lax.all_gather(u_panels, "row", axis=3, tiled=True)[0, :, 0]
+    col_panel = collect(u_panels, "row", 3)[0, :, 0]
     col_targets = jnp.arange(col_count, dtype=jnp.int32)
     col_hot = (col_map[:, :, None] == col_targets[None, None, :]).astype(jnp.float32)
     col_dense = jnp.einsum("hjg,hjk->hgk", col_hot, col_panel, precision=lax.Precision.HIGHEST)

time: 146 us -> 146 us (level)
  blocking collectives: 12.5 us -> 0 us
  waiting for transfers between devices: 102 us -> 108 us
  starting transfers between devices: 0.04 us -> 4.83 us
  local copies, waits for them, and re-layouts: 0.73 us -> 2.62 us
    all_gather x1 -> x0, blocking collectives: 12.5 us -> none  [shards(): col_panel = lax.all_gather(u_panels, 'row', axis=3, tiled=True)[0, :, 0]]
    ppermute x0 -> x3, waiting for transfers between devices: none -> 5.47 us  [the longest x2 5.47 us: collect(): earlier.append(lax.ppermute(earlier[-1], axis, up))]
    ppermute x0 -> x3, starting transfers between devices: none -> 4.79 us  [the longest x1 2.49 us: collect(): later.append(lax.ppermute(later[-1], axis, down))]
    unnamed x3 -> x10, local copies, waits for them, and re-layouts: 0.73 us -> 2.61 us
  transfers between devices with their start and end apart: 2 -> 5, of which waited for: 2 -> 4; matrix products, arithmetic and copies ran while one was open for 2% -> 3% of each run, Pallas kernels for 0% -> 0%
where the time goes in v1:
time: 146 us
  waiting for transfers between devices  108 us (74%)
  matrix products  15.3 us (10%)
  between operations  13.5 us (9%)
  starting transfers between devices  4.83 us (3%)
  local copies, waits for them, and re-layouts  2.62 us (2%)
  other arithmetic  1.89 us (1%)
    all_gather x1, waiting for transfers between devices, shards(): row_panel = lax.all_gather(l_panels, 'col', axis=3, tiled=True)[0, :, 0]  71.1 us
    psum x1, waiting for transfers between devices, shards(): summed = lax.psum(update, 'gz')  30.3 us
    dot_general x1, matrix products, spread_dense(): jnp.einsum('hif,hig->fg', row_hot, narrow, precision=lax.Precision.HIGHEST)  8.37 us
    ppermute x2, waiting for transfers between devices, collect(): earlier.append(lax.ppermute(earlier[-1], axis, up))  5.47 us
    dot_general x1, matrix products, spread_dense(): jnp.einsum('hik,hgk->hig', row_panel, col_dense, precision=lax.Precision....  5.34 us
  transfers between devices with their start and end apart: 5, of which 4 were waited for; matrix products, arithmetic and copies ran while one was open for 3% of the time, Pallas kernels for 0%

profile of v1, /device:TPU:1, one launch (start us, length us, event | category | flops | bytes accessed | tf_op | source)
XLA Modules:
  0.0 145.7 jit_solution(486036263171237921)
XLA Ops:
  6.5 0.0 all-gather.2.cloned.1.call-start
  6.5 0.7 all-gather.2.cloned.1.call-update
  7.3 0.0 all-reduce.2.cloned.1.call-start
  7.3 2.1 %collective-permute-start = (f32[1,8,1,16,256]{4,3,2,1,0:T(8,128)}, f32[1,8,1,16,256]{4,3,2,1,0:T(8,128)S(1)}, u32[]{:S(2)}, u32[]{:S(2)}) collective-permute-start(f32[1,8,1,16,256]{4,3,2,1,0:T(8,128)} %param.8), channel_id=1, source_target_pairs={{0,32},{32,64},{64,96},{96,0},{1,33},{33,65},{65,97},{97,1},{2,34}... | collective-permute-start | bytes 393224 | tf_op jit(solution)/shard_map/ppermute | solution.py:13
  9.4 3.8 %collective-permute-done = f32[1,8,1,16,256]{4,3,2,1,0:T(8,128)S(1)} collective-permute-done((f32[1,8,1,16,256]{4,3,2,1,0:T(8,128)}, f32[1,8,1,16,256]{4,3,2,1,0:T(8,128)S(1)}, u32[]{:S(2)}, u32[]{:S(2)}) %collective-permute-start) | collective-permute-done | bytes 131104 | tf_op jit(solution)/shard_map/ppermute | solution.py:13
  13.3 0.2 collective-permute-start.1
  13.4 2.5 %collective-permute-start.2 = (f32[1,8,1,16,256]{4,3,2,1,0:T(8,128)}, f32[1,8,1,16,256]{4,3,2,1,0:T(8,128)S(1)}, u32[]{:S(2)}, u32[]{:S(2)}) collective-permute-start(f32[1,8,1,16,256]{4,3,2,1,0:T(8,128)} %param.8), channel_id=1, source_target_pairs={{0,96},{32,0},{64,32},{96,64},{1,97},{33,1},{65,33},{97,65},{2,98}... | collective-permute-start | bytes 393224 | tf_op jit(solution)/shard_map/ppermute | solution.py:15
  15.9 0.7 copy.8
  16.7 1.6 %collective-permute-done.1 = f32[1,8,1,16,256]{4,3,2,1,0:T(8,128)S(1)} collective-permute-done((f32[1,8,1,16,256]{4,3,2,1,0:T(8,128)S(1)}, f32[1,8,1,16,256]{4,3,2,1,0:T(8,128)S(1)}, u32[]{:S(2)}, u32[]{:S(2)}) %collective-permute-start.1) | collective-permute-done | bytes 131104 | tf_op jit(solution)/shard_map/ppermute | solution.py:13
  18.3 0.9 constant_dynamic-update-slice_fusion.5
  19.2 0.0 collective-permute-done.2
  19.3 0.9 constant_dynamic-update-slice_fusion.1
  20.2 1.6 %fusion.8 = f32[8,128,256]{2,1,0:T(8,128)S(1)} fusion(f32[1,8,1,128,256]{4,3,2,1,0:T(8,128)S(1)} %constant_dynamic-update-slice_fusion, s32[]{:T(128)S(6)} %select_n.14, s32[8,64]{1,0:T(8,128)} %bitcast.19), kind=kOutput, calls=%fused_computation.7 | convolution fusion | flops 201392128 | bytes 1574916 | tf_op jit(solution)/shard_map/hjg,hjk->hgk/dot_general | solution.py:34
  21.8 71.1 %all-gather.2.cloned.1.call-done = f32[1,8,1,512,256]{4,3,2,1,0:T(8,128)} async-done(((f32[1,8,1,16,256]{4,3,2,1,0:T(8,128)}), f32[1,8,1,512,256]{4,3,2,1,0:T(8,128)}) %all-gather.2.cloned.1.call-update) | async-done | bytes 4194320 | tf_op jit(solution)/shard_map/all_gather | solution.py:35
  92.9 5.3 %fusion.2 = f32[8,128,512]{1,2,0:T(8,128)S(1)} fusion(f32[8,128,256]{2,1,0:T(8,128)S(1)} %fusion.8, f32[1,8,1,512,256]{4,3,2,1,0:T(8,128)} %all-gather.2.cloned.1.call-done), kind=kOutput, calls=%fused_computation.3 | convolution fusion | flops 1610612736 | bytes 7340032 | tf_op jit(solution)/shard_map/hik,hgk->hig/dot_general | solution.py:22
  98.3 0.0 copy-start
  98.3 8.4 %fusion.5 = f32[1024,128]{1,0:T(8,128)} fusion(f32[8,128,512]{1,2,0:T(8,128)S(1)} %fusion.2, s32[8,512]{1,0:T(8,128)S(1)} %bitcast.18), kind=kOutput, calls=%fused_computation.6 | convolution fusion | flops 6446645248 | bytes 2637824 | tf_op jit(solution)/shard_map/hif,hig->fg/dot_general | solution.py:24
  106.6 0.0 all-reduce.2.cloned.1.call-update
  106.7 30.3 %all-reduce.2.cloned.1.call-done = f32[1024,128]{1,0:T(8,128)} async-done(((f32[1024,128]{1,0:T(8,128)}), f32[1024,128]{1,0:T(8,128)}) %all-reduce.2.cloned.1.call-update) | async-done | bytes 524304 | tf_op jit(solution)/shard_map/psum | solution.py:37
  137.0 0.0 copy-done
  137.0 1.9 %sub.12 = f32[1024,128]{1,0:T(8,128)} subtract(f32[1024,128]{1,0:T(8,128)S(1)} %copy-done, f32[1024,128]{1,0:T(8,128)} %all-reduce.2.cloned.1.call-done) | non-fusion elementwise | flops 131072 | bytes 1572864 | tf_op jit(solution)/shard_map/sub | solution.py:38
  (6 shorter events, 0.1 us)
Async XLA Ops:
  6.5 86.4 %all-gather.2.cloned.1.call-start = ((), (), s32[]{:S(2)}) async-start(), calls=%async_computation | async-start | bytes 4325376 | tf_op jit(solution)/shard_map/all_gather | solution.py:35
  7.3 129.7 %all-reduce.2.cloned.1.call-start = ((), (), s32[]{:S(2)}) async-start(), calls=%async_computation.1 | async-start | bytes 1048576 | tf_op jit(solution)/shard_map/psum | solution.py:37
  7.3 6.0 %collective-permute-start = (f32[1,8,1,16,256]{4,3,2,1,0:T(8,128)}, f32[1,8,1,16,256]{4,3,2,1,0:T(8,128)S(1)}, u32[]{:S(2)}, u32[]{:S(2)}) collective-permute-start(f32[1,8,1,16,256]{4,3,2,1,0:T(8,128)} %param.8), channel_id=1, source_target_pairs={{0,32},{32,64},{64,96},{96,0},{1,33},{33,65},{65,97},{97,1},{2,34}... | collective-permute-start | bytes 393224 | tf_op jit(solution)/shard_map/ppermute | solution.py:13
  13.3 5.0 %collective-permute-start.1 = (f32[1,8,1,16,256]{4,3,2,1,0:T(8,128)S(1)}, f32[1,8,1,16,256]{4,3,2,1,0:T(8,128)S(1)}, u32[]{:S(2)}, u32[]{:S(2)}) collective-permute-start(f32[1,8,1,16,256]{4,3,2,1,0:T(8,128)S(1)} %collective-permute-done), channel_id=1, source_target_pairs={{0,32},{32,64},{64,96},{96,0},{1,33},{33,65},{65,97},{97,1},{2,34}... | collective-permute-start | bytes 393224 | tf_op jit(solution)/shard_map/ppermute | solution.py:13
  13.4 5.8 %collective-permute-start.2 = (f32[1,8,1,16,256]{4,3,2,1,0:T(8,128)}, f32[1,8,1,16,256]{4,3,2,1,0:T(8,128)S(1)}, u32[]{:S(2)}, u32[]{:S(2)}) collective-permute-start(f32[1,8,1,16,256]{4,3,2,1,0:T(8,128)} %param.8), channel_id=1, source_target_pairs={{0,96},{32,0},{64,32},{96,64},{1,97},{33,1},{65,33},{97,65},{2,98}... | collective-permute-start | bytes 393224 | tf_op jit(solution)/shard_map/ppermute | solution.py:15
  98.3 38.7 %copy-start = (f32[1024,128]{1,0:T(8,128)S(1)}, f32[1024,128]{1,0:T(8,128)}, u32[]{:S(2)}) copy-start(f32[1024,128]{1,0:T(8,128)} %param.5) | copy-start | bytes 1572868
Sparse Core Ops, SparseCore 0:
  9.9 82.9 all-gather.1
  106.8 30.1 all-reduce.1

commit v2 on v0

--- a/solution.py
+++ b/solution.py
@@ -21,7 +21,7 @@
     col_dense = jnp.einsum("hjg,hjk->hgk", col_hot, col_panel, precision=lax.Precision.HIGHEST)
     row_panel = lax.all_gather(l_panels, "col", axis=3, tiled=True)[0, :, 0]
     update = spread_dense(row_panel, row_map, col_dense, row_count)
-    summed = lax.psum(update, "gz")
+    summed = jnp.sum(lax.all_gather(update, "gz"), axis=0)
     return front_matrix - summed
 
 

time: 146 us -> 131 us (0.90)
  waiting for transfers between devices: 102 us -> 86.7 us
    psum x1 -> x0, waiting for transfers between devices: 30.3 us -> none  [shards(): summed = lax.psum(update, 'gz')]
    all_gather x0 -> x1, waiting for transfers between devices: none -> 15.1 us  [shards(): summed = jnp.sum(lax.all_gather(update, 'gz'), axis=0)]
where the time goes in v2:
time: 131 us
  waiting for transfers between devices  86.7 us (66%)
  matrix products  15.3 us (12%)
  between operations  13.4 us (10%)
  blocking collectives  12.5 us (10%)
  other arithmetic  2.19 us (2%)
    all_gather x1, waiting for transfers between devices, shards(): row_panel = lax.all_gather(l_panels, 'col', axis=3, tiled=True)[0, :, 0]  70.8 us
    all_gather x1, waiting for transfers between devices, shards(): summed = jnp.sum(lax.all_gather(update, 'gz'), axis=0)  15.1 us
    all_gather x1, blocking collectives, shards(): col_panel = lax.all_gather(u_panels, 'row', axis=3, tiled=True)[0, :, 0]  12.5 us
    dot_general x1, matrix products, spread_dense(): jnp.einsum('hif,hig->fg', row_hot, narrow, precision=lax.Precision.HIGHEST)  8.37 us
    dot_general x1, matrix products, spread_dense(): jnp.einsum('hik,hgk->hig', row_panel, col_dense, precision=lax.Precision....  5.34 us
  transfers between devices with their start and end apart: 2, of which 2 were waited for; matrix products, arithmetic and copies ran while one was open for 2% of the time, Pallas kernels for 0%

profile of v2, /device:TPU:1, one launch (start us, length us, event | category | flops | bytes accessed | tf_op | source)
XLA Modules:
  0.0 130.9 jit_solution(11324993893138850321)
XLA Ops:
  6.5 0.0 all-gather.4.cloned.1.call-start
  6.5 0.7 all-gather.4.cloned.1.call-update
  7.3 0.0 all-gather.6.cloned.1.call-start
  7.3 0.7 copy.8
  8.0 12.5 %all_gather.12 = f32[1,8,1,64,256]{4,3,2,1,0:T(8,128)S(1)} all-gather(f32[1,8,1,16,256]{4,3,2,1,0:T(8,128)} %param.8), channel_id=1, replica_groups=mesh['gz'=2,'row'=4,'col'=32] {'row'}, dimensions={3}, use_global_device_ids=true | all-gather | bytes 655360 | tf_op jit(solution)/shard_map/all_gather | solution.py:18
  20.6 1.5 %fusion.8 = f32[8,128,256]{2,1,0:T(8,128)S(1)} fusion(f32[1,8,1,64,256]{4,3,2,1,0:T(8,128)S(1)} %all_gather.12, s32[8,64]{1,0:T(8,128)} %bitcast.21), kind=kOutput, calls=%fused_computation.7 | convolution fusion | flops 201392128 | bytes 1574912 | tf_op jit(solution)/shard_map/hjg,hjk->hgk/dot_general | solution.py:21
  22.1 70.8 %all-gather.4.cloned.1.call-done = f32[1,8,1,512,256]{4,3,2,1,0:T(8,128)} async-done(((f32[1,8,1,16,256]{4,3,2,1,0:T(8,128)}), f32[1,8,1,512,256]{4,3,2,1,0:T(8,128)}) %all-gather.4.cloned.1.call-update) | async-done | bytes 4194320 | tf_op jit(solution)/shard_map/all_gather | solution.py:22
  92.9 5.3 %fusion.2 = f32[8,128,512]{1,2,0:T(8,128)S(1)} fusion(f32[8,128,256]{2,1,0:T(8,128)S(1)} %fusion.8, f32[1,8,1,512,256]{4,3,2,1,0:T(8,128)} %all-gather.4.cloned.1.call-done), kind=kOutput, calls=%fused_computation.3 | convolution fusion | flops 1610612736 | bytes 7340032 | tf_op jit(solution)/shard_map/hik,hgk->hig/dot_general | solution.py:9
  98.3 0.0 copy-start
  98.3 8.4 %fusion.5 = f32[1024,128]{1,0:T(8,128)} fusion(f32[8,128,512]{1,2,0:T(8,128)S(1)} %fusion.2, s32[8,512]{1,0:T(8,128)S(1)} %bitcast.20), kind=kOutput, calls=%fused_computation.6 | convolution fusion | flops 6446645248 | bytes 2637824 | tf_op jit(solution)/shard_map/hif,hig->fg/dot_general | solution.py:11
  106.6 0.0 all-gather.6.cloned.1.call-update
  106.7 15.1 %all-gather.6.cloned.1.call-done = f32[2048,128]{1,0:T(8,128)} async-done(((f32[1024,128]{1,0:T(8,128)}), f32[2048,128]{1,0:T(8,128)}) %all-gather.6.cloned.1.call-update) | async-done | bytes 1048592 | tf_op jit(solution)/shard_map/all_gather | solution.py:24
  121.8 1.3 %reduce_sum.9 = f32[1024,128]{1,0:T(8,128)S(1)} reduce(f32[2,1024,128]{2,1,0:T(8,128)} %bitcast.19, f32[]{:T(128)} %constant.0.clone.1), dimensions={0}, to_apply=%region_0.0 | reduce | flops 131072 | bytes 1572868 | tf_op jit(solution)/shard_map/reduce_sum | solution.py:24
  123.2 0.0 copy-done
  123.2 0.8 sub.3
Async XLA Ops:
  6.5 86.4 %all-gather.4.cloned.1.call-start = ((), (), s32[]{:S(2)}) async-start(), calls=%async_computation | async-start | bytes 4325376 | tf_op jit(solution)/shard_map/all_gather | solution.py:22
  7.3 114.6 %all-gather.6.cloned.1.call-start = ((), (), s32[]{:S(2)}) async-start(), calls=%async_computation.1 | async-start | bytes 1572864 | tf_op jit(solution)/shard_map/all_gather | solution.py:24
  98.3 24.9 %copy-start = (f32[1024,128]{1,0:T(8,128)S(1)}, f32[1024,128]{1,0:T(8,128)}, u32[]{:S(2)}) copy-start(f32[1024,128]{1,0:T(8,128)} %param.5) | copy-start | bytes 1572868
Sparse Core Ops, SparseCore 0:
  9.9 82.9 all-gather.3
  106.8 14.9 all-gather.5
